TPU v7x, 128 devices: a whole 4x4x4 slice. The times are simulated.
128 devices in a mesh: ray: 16 (over x, z), tile: 8 (over y, core).
Axes of the slice: x: 4, y: 4, z: 4, core: 2. Of those that a mesh axis runs over, the one named last changes fastest.
Arguments:
- data: float32 [64, 262144], P(None, ('ray', 'tile')), may hold values from -6 to 6
- sensitivity: bfloat16 [4096, 256, 512], P(('ray', 'tile')), may hold values from -0.25 to 0.25
- block_tiles: int32 [128, 8, 4], P(('ray', 'tile')), may hold values from 0 to 47
- block_bundles: int32 [128, 8, 4], P(('ray', 'tile')), may hold values from 0 to 7
Outputs:
- solution: float32 [64, 196608], P(None, 'tile')
- residual: float32 [64, 262144], P(None, ('ray', 'tile'))
Inputs may be any that keep to these rules, and one draw needn't show every extreme that they name: `block_tiles`: position of the block's tile among the 48 tiles of the owner given by the second index. `block_bundles`: the block's ray bundle among the device's 8 bundles.
All inputs are finite; a program needn't handle non-finite values.
Results may differ from a plain program's by a relative error of at most 0.004.
The roundings to bfloat16 on the way count: a program that leaves them out, or rounds other values in their place, can miss the bound.
Values may be sent and summed in bfloat16 or wider, within the bound.
A program may use at most 128 MiB of HBM per device.

v0:
```python
import jax
import jax.numpy as jnp
from jax import lax
from jax.sharding import PartitionSpec as P

RB = 256
CB = 512
ITERS = 2
BUND_DEV = 8
TILE_DEV = 48
eps_norm = 1e-06


def per_device(data, sensitivity, block_tiles, block_bundles):
    columns = data.shape[0]
    bundles = block_bundles.reshape(-1)
    requests = lax.all_to_all(block_tiles, "tile", split_axis=1, concat_axis=1, tiled=True).reshape(
        -1
    )
    bundle_onehot = (bundles[:, None] == jnp.arange(BUND_DEV, dtype=jnp.int32)[None, :]).astype(
        jnp.float32
    )
    owner_onehot = (requests[:, None] == jnp.arange(TILE_DEV, dtype=jnp.int32)[None, :]).astype(
        jnp.bfloat16
    )

    def fetch(field_bf):
        owned = field_bf.reshape(columns, TILE_DEV, CB)
        outgoing = jnp.take(owned, requests, axis=1)
        tiles = lax.all_to_all(outgoing, "tile", split_axis=1, concat_axis=1, tiled=True)
        return tiles

    def forward(field_bf):
        tiles = fetch(field_bf)
        partial_value = jnp.einsum(
            "cnk,nrk->ncr", tiles, sensitivity, preferred_element_type=jnp.float32
        )
        summed = jnp.einsum(
            "ncr,nb->cbr", partial_value, bundle_onehot, precision=lax.Precision.HIGHEST
        )
        return summed.reshape(columns, BUND_DEV * RB)

    def adjoint(rays_bf):
        picked = jnp.take(rays_bf.reshape(columns, BUND_DEV, RB), bundles, axis=1)
        terms = jnp.einsum(
            "cnr,nrk->cnk", picked, sensitivity, preferred_element_type=jnp.float32
        ).astype(jnp.bfloat16)
        arrived = lax.all_to_all(terms, "tile", split_axis=1, concat_axis=1, tiled=True)
        owned = jnp.einsum(
            "cnk,nt->ctk", arrived, owner_onehot, preferred_element_type=jnp.float32
        ).reshape(columns, TILE_DEV * CB)
        total = lax.psum(owned, "ray")
        return total

    def cell_norm(field):
        local = jnp.sum(field * field, axis=1)
        total = lax.psum(local, "tile")
        return jnp.sqrt(total + eps_norm)

    def ray_norm(rays):
        total = lax.psum(jnp.sum(rays * rays, axis=1), ("ray", "tile"))
        return jnp.sqrt(total + eps_norm)

    beta_now = ray_norm(data)
    rays_dir = data / beta_now[:, None]
    model_dir = adjoint(rays_dir.astype(jnp.bfloat16))
    alpha_now = cell_norm(model_dir)
    model_dir = model_dir / alpha_now[:, None]
    search = model_dir
    solution = jnp.zeros_like(model_dir)
    phi_bar = beta_now
    rho_bar = alpha_now
    for step in range(ITERS):
        rounded = model_dir.astype(jnp.bfloat16)
        rays_dir = forward(rounded) - alpha_now[:, None] * rays_dir
        beta_now = ray_norm(rays_dir)
        rays_dir = rays_dir / beta_now[:, None]
        rho_now = jnp.sqrt(rho_bar * rho_bar + beta_now * beta_now)
        cosine = rho_bar / rho_now
        sine_part = beta_now / rho_now
        phi_now = cosine * phi_bar
        phi_bar = sine_part * phi_bar
        solution = solution + (phi_now / rho_now)[:, None] * search
        if step + 1 < ITERS:
            model_dir = adjoint(rays_dir.astype(jnp.bfloat16)) - beta_now[:, None] * model_dir
            alpha_now = cell_norm(model_dir)
            model_dir = model_dir / alpha_now[:, None]
            theta_now = sine_part * alpha_now
            rho_bar = -cosine * alpha_now
            search = model_dir - (theta_now / rho_now)[:, None] * search
    residual = data - forward(solution.astype(jnp.bfloat16))
    return (solution, residual)


def solution(mesh):
    return jax.shard_map(
        per_device,
        mesh=mesh,
        in_specs=(
            P(None, ("ray", "tile")),
            P(("ray", "tile"), None, None),
            P(("ray", "tile"), None, None),
            P(("ray", "tile"), None, None),
        ),
        out_specs=(P(None, "tile"), P(None, ("ray", "tile"))),
        check_vma=False,
    )
```

profile of v0, /device:TPU:1, one launch (start us, length us, event | category | flops | bytes accessed | tf_op | source)
XLA Modules:
  0.0 731.6 jit_solution(17410393598439722855)
XLA Ops:
  8.5 6.0 all-to-all-start
  16.5 67.7 %psum.49 = f32[64]{0:T(128)S(1)} all-reduce(f32[64]{0:T(128)S(1)} %multiply_reduce_fusion.4), channel_id=1, replica_groups=mesh['ray'=16,'tile'=8] {'ray','tile'}, use_global_device_ids=true, to_apply=%region_1.0 | all-reduce | flops 64 | bytes 512 | tf_op jit(solution)/shard_map/psum | solution.py:61
  86.1 6.3 convert_bitcast_fusion.1
  92.4 4.4 all-to-all-start.1
  98.1 25.1 %all-to-all-done.1 = bf16[64,32,512]{2,0,1:T(8,128)(2,1)S(1)} async-done(((bf16[64,32,512]{2,0,1:T(8,128)(2,1)}), bf16[64,32,512]{2,0,1:T(8,128)(2,1)S(1)}, u32[]{:S(2)}, u32[]{:S(2)}) %all-to-all-start.1) | async-done | bytes 2097184 | tf_op jit(solution)/shard_map/all_to_all | solution.py:48
  124.9 6.3 copy.39
  131.3 119.1 %all-reduce.3.cloned.1.call-done = f32[64,24576]{1,0:T(8,128)} async-done(((f32[64,24576]{1,0:T(8,128)}), f32[64,24576]{1,0:T(8,128)}) %all-reduce.3.cloned.1.call-update) | async-done | bytes 6291472 | tf_op jit(solution)/shard_map/psum | solution.py:52
  253.7 12.4 %psum.51 = f32[64]{0:T(128)S(1)} all-reduce(f32[64]{0:T(128)S(1)} %multiply_reduce_fusion.1), channel_id=1, replica_groups=mesh['ray'=16,'tile'=8] {'tile'}, use_global_device_ids=true, to_apply=%region_4.6 | all-reduce | flops 64 | bytes 512 | tf_op jit(solution)/shard_map/psum | solution.py:57
  273.7 31.7 %all_to_all.30 = bf16[64,32,512]{2,0,1:T(8,128)(2,1)S(1)} all-to-all(bf16[64,32,512]{2,0,1:T(8,128)(2,1)S(1)} %select_bitcast_fusion.2), channel_id=1, replica_groups=mesh['ray'=16,'tile'=8] {'tile'}, dimensions={1} | all-to-all | bytes 4194304 | tf_op jit(solution)/shard_map/all_to_all | solution.py:30
  305.4 6.0 fusion.41
  313.9 64.5 %psum.52 = f32[64]{0:T(128)S(1)} all-reduce(f32[64]{0:T(128)S(1)} %get-tuple-element.11), channel_id=1, replica_groups=mesh['ray'=16,'tile'=8] {'ray','tile'}, use_global_device_ids=true, to_apply=%region_6.0 | all-reduce | flops 64 | bytes 512 | tf_op jit(solution)/shard_map/psum | solution.py:61
  379.2 5.0 convert_bitcast_fusion
  384.2 30.1 %all_to_all.31 = bf16[64,32,512]{2,0,1:T(8,128)(2,1)S(1)} all-to-all(bf16[64,32,512]{2,0,1:T(8,128)(2,1)S(1)} %convert_bitcast_fusion), channel_id=1, replica_groups=mesh['ray'=16,'tile'=8] {'tile'}, dimensions={1} | all-to-all | bytes 4194304 | tf_op jit(solution)/shard_map/all_to_all | solution.py:48
  416.0 6.3 copy.41
  422.3 118.9 %all-reduce.5.cloned.1.call-done = f32[64,24576]{1,0:T(8,128)} async-done(((f32[64,24576]{1,0:T(8,128)}), f32[64,24576]{1,0:T(8,128)}) %all-reduce.5.cloned.1.call-update) | async-done | bytes 6291472 | tf_op jit(solution)/shard_map/psum | solution.py:52
  541.2 5.8 multiply_reduce_fusion
  547.0 12.4 %psum.54 = f32[64]{0:T(128)S(1)} all-reduce(f32[64]{0:T(128)S(1)} %multiply_reduce_fusion), channel_id=1, replica_groups=mesh['ray'=16,'tile'=8] {'tile'}, use_global_device_ids=true, to_apply=%region_9.12 | all-reduce | flops 64 | bytes 512 | tf_op jit(solution)/shard_map/psum | solution.py:57
  559.4 5.2 fusion.10
  568.9 31.7 %all_to_all.32 = bf16[64,32,512]{2,0,1:T(8,128)(2,1)S(1)} all-to-all(bf16[64,32,512]{2,0,1:T(8,128)(2,1)S(1)} %select_bitcast_fusion.1), channel_id=1, replica_groups=mesh['ray'=16,'tile'=8] {'tile'}, dimensions={1} | all-to-all | bytes 4194304 | tf_op jit(solution)/shard_map/all_to_all | solution.py:30
  600.7 6.0 fusion.42
  609.1 64.8 %psum.55 = f32[64]{0:T(128)S(1)} all-reduce(f32[64]{0:T(128)S(1)} %multiply_reduce_fusion.2), channel_id=1, replica_groups=mesh['ray'=16,'tile'=8] {'ray','tile'}, use_global_device_ids=true, to_apply=%region_11.14 | all-reduce | flops 64 | bytes 512 | tf_op jit(solution)/shard_map/psum | solution.py:61
  673.9 7.4 %fusion.38 = (bf16[64,24576]{1,0:T(8,128)(2,1)S(1)}, f32[64,24576]{1,0:T(8,128)}) fusion(f32[64]{0:T(128)S(1)} %multiply_divide_fusion, f32[64]{0:T(128)S(1)} %add_sqrt_fusion, f32[64,24576]{1,0:T(8,128)} %all-reduce.5.cloned.1.call-done, f32[64]{0:T(128)S(1)} %get-tuple-element.13, f32[64]{0:T(128)S(1)} %get-tuple-element.9, ...), kind=kLoop, calls=%fused_computation.76 | loop fusion | flops 15728640 | bytes 22021632 | tf_op jit(solution)/shard_map/convert_element_type | solution.py:91
  685.6 30.1 %all_to_all.33 = bf16[64,32,512]{2,0,1:T(8,128)(2,1)S(1)} all-to-all(bf16[64,32,512]{2,0,1:T(8,128)(2,1)S(1)} %select_bitcast_fusion), channel_id=1, replica_groups=mesh['ray'=16,'tile'=8] {'tile'}, dimensions={1} | all-to-all | bytes 4194304 | tf_op jit(solution)/shard_map/all_to_all | solution.py:30
  715.7 6.0 fusion.43
  (60 shorter events, 37.9 us)
Async XLA Ops:
  8.5 83.9 %all-to-all-start = ((s32[1,8,4]{2,0,1:T(1,128)}), s32[1,8,4]{2,0,1:T(1,128)S(1)}, u32[]{:S(2)}, u32[]{:S(2)}) async-start(s32[1,8,4]{2,0,1:T(1,128)} %copy.22), calls=%async_computation | async-start | bytes 8192 | tf_op jit(solution)/shard_map/all_to_all | solution.py:17
  92.4 30.8 %all-to-all-start.1 = ((bf16[64,32,512]{2,0,1:T(8,128)(2,1)}), bf16[64,32,512]{2,0,1:T(8,128)(2,1)S(1)}, u32[]{:S(2)}, u32[]{:S(2)}) async-start(bf16[64,32,512]{2,0,1:T(8,128)(2,1)} %convert_bitcast_fusion.1), calls=%async_computation.1 | async-start | bytes 4194304 | tf_op jit(solution)/shard_map/all_to_all | solution.py:48
  96.8 153.6 %all-reduce.3.cloned.1.call-start = ((), (), s32[]{:S(2)}) async-start(), calls=%async_computation.6 | async-start | bytes 12582912 | tf_op jit(solution)/shard_map/psum | solution.py:52
  131.2 410.0 %all-reduce.5.cloned.1.call-start = ((), (), s32[]{:S(2)}) async-start(), calls=%async_computation.7 | async-start | bytes 12582912 | tf_op jit(solution)/shard_map/psum | solution.py:52
  311.4 2.1 copy-start
  313.9 64.7 %copy-start.2 = (f32[64,2048]{1,0:T(8,128)}, f32[64,2048]{1,0:T(8,128)S(1)}, u32[]{:S(2)}) copy-start(f32[64,2048]{1,0:T(8,128)S(1)} %get-tuple-element.12) | copy-start | bytes 1572868
  606.7 2.1 copy-start.3
  721.7 2.1 copy-start.1
Sparse Core Ops, SparseCore 0:
  131.3 119.0 all-reduce.2
  422.4 118.6 all-reduce.4
where the time goes:
time: 733 us; the launch traced here: 732 us
  blocking collectives  346 us (47%)
  waiting for transfers between devices  263 us (36%)
  matrix products  38.8 us (5%)
  other arithmetic  35 us (5%)
  local copies, waits for them, and re-layouts  24.4 us (3%)
  between operations  14.3 us (2%)
  starting transfers between devices  10.4 us (1%)
    psum x2, waiting for transfers between devices, adjoint(): total = lax.psum(owned, 'ray')  238 us
    psum x3, blocking collectives, ray_norm(): total = lax.psum(jnp.sum(rays * rays, axis=1), ('ray', 'tile'))  197 us
    all_to_all x3, blocking collectives, fetch(): lax.all_to_all(outgoing, 'tile', split_axis=1, concat_axis=1, tiled=True)  93.6 us
    all_to_all x1, blocking collectives, adjoint(): lax.all_to_all(terms, 'tile', split_axis=1, concat_axis=1, tiled=True)  30.1 us
    all_to_all x1, waiting for transfers between devices, adjoint(): lax.all_to_all(terms, 'tile', split_axis=1, concat_axis=1, tiled=True)  25.1 us
    psum x2, blocking collectives, cell_norm(): total = lax.psum(local, 'tile')  24.9 us
    dot_general x3, matrix products, forward(): jnp.einsum('cnk,nrk->ncr', tiles, sensitivity, preferred_element_type=jnp...  18.1 us
    unnamed x15, local copies, waits for them, and re-layouts  15.1 us
  transfers between devices with their start and end apart: 4, of which 3 were waited for; matrix products, arithmetic and copies ran while one was open for 2% of the time, Pallas kernels for 0%

commit v1 on v0

--- a/solution.py
+++ b/solution.py
@@ -49,7 +49,8 @@
         owned = jnp.einsum(
             "cnk,nt->ctk", arrived, owner_onehot, preferred_element_type=jnp.float32
         ).reshape(columns, TILE_DEV * CB)
-        total = lax.psum(owned, "ray")
+        parts = lax.all_gather(owned, "ray")
+        total = jnp.sum(parts, axis=0)
         return total
 
     def cell_norm(field):

time: 733 us -> 1640 us (2.24)
  waiting for transfers between devices: 263 us -> 1120 us
  other arithmetic: 35 us -> 110 us
  blocking collectives: 346 us -> 316 us
    all_gather x0 -> x2, waiting for transfers between devices: none -> 1070 us  [adjoint(): parts = lax.all_gather(owned, 'ray')]
    psum x2 -> x0, waiting for transfers between devices: 238 us -> none  [adjoint(): total = lax.psum(owned, 'ray')]
    reduce_sum x0 -> x2, other arithmetic: none -> 67.1 us  [adjoint(): total = jnp.sum(parts, axis=0)]
    all_to_all x3 -> x2, blocking collectives: 93.6 us -> 63.5 us  [fetch(): lax.all_to_all(outgoing, 'tile', split_axis=1, concat_axis=1, tiled=True)]
    all_to_all x0 -> x1, waiting for transfers between devices: none -> 19 us  [fetch(): lax.all_to_all(outgoing, 'tile', split_axis=1, concat_axis=1, tiled=True)]
  transfers between devices with their start and end apart: 4 -> 5, of which waited for: 3 -> 4; matrix products, arithmetic and copies ran while one was open for 2% -> 1% of each run, Pallas kernels for 0% -> 0%
where the time goes in v1:
time: 1640 us
  waiting for transfers between devices  1120 us (68%)
  blocking collectives  316 us (19%)
  other arithmetic  110 us (7%)
  matrix products  44.2 us (3%)
  local copies, waits for them, and re-layouts  23 us (1%)
    all_gather x2, waiting for transfers between devices, adjoint(): parts = lax.all_gather(owned, 'ray')  1070 us
    psum x3, blocking collectives, ray_norm(): total = lax.psum(jnp.sum(rays * rays, axis=1), ('ray', 'tile'))  197 us
    reduce_sum x2, other arithmetic, adjoint(): total = jnp.sum(parts, axis=0)  67.1 us
    all_to_all x2, blocking collectives, fetch(): lax.all_to_all(outgoing, 'tile', split_axis=1, concat_axis=1, tiled=True)  63.5 us
  transfers between devices with their start and end apart: 5, of which 4 were waited for; matrix products, arithmetic and copies ran while one was open for 1% of the time, Pallas kernels for 0%

profile of v1, /device:TPU:1, one launch (start us, length us, event | category | flops | bytes accessed | tf_op | source)
XLA Modules:
  0.0 1638.3 jit_solution(7632157956531530285)
XLA Ops:
  8.5 6.0 all-to-all-start
  16.5 67.7 %psum.35 = f32[64]{0:T(128)S(1)} all-reduce(f32[64]{0:T(128)S(1)} %multiply_reduce_fusion.4), channel_id=1, replica_groups=mesh['ray'=16,'tile'=8] {'ray','tile'}, use_global_device_ids=true, to_apply=%region_1.0 | all-reduce | flops 64 | bytes 512 | tf_op jit(solution)/shard_map/psum | solution.py:62
  86.1 6.3 convert_bitcast_fusion.1
  98.0 25.1 %all-to-all-done.1 = bf16[64,32,512]{2,0,1:T(8,128)(2,1)S(1)} async-done(((bf16[64,32,512]{2,0,1:T(8,128)(2,1)}), bf16[64,32,512]{2,0,1:T(8,128)(2,1)S(1)}, u32[]{:S(2)}, u32[]{:S(2)}) %all-to-all-start.1) | async-done | bytes 2097184 | tf_op jit(solution)/shard_map/all_to_all | solution.py:48
  127.6 6.2 all_gather_reshape.6
  133.9 536.2 %all-gather.3.cloned.1.call-done = f32[16,64,24576]{2,1,0:T(8,128)} async-done(((f32[1,64,24576]{2,1,0:T(8,128)}), f32[16,64,24576]{2,1,0:T(8,128)}) %all-gather.3.cloned.1.call-update) | async-done | bytes 100663312 | tf_op jit(solution)/shard_map/all_gather | solution.py:52
  670.1 33.6 %reduce_sum.68 = f32[64,24576]{1,0:T(8,128)} reduce(f32[16,64,24576]{2,1,0:T(8,128)} %all-gather.3.cloned.1.call-done, f32[]{:T(128)} %constant.18.clone.1), dimensions={0}, to_apply=%region_2.0 | reduce | flops 23592960 | bytes 106954752 | tf_op jit(solution)/shard_map/reduce_sum | solution.py:53
  707.0 12.4 psum.36
  727.1 31.7 %all_to_all.30 = bf16[64,32,512]{2,0,1:T(8,128)(2,1)S(1)} all-to-all(bf16[64,32,512]{2,0,1:T(8,128)(2,1)S(1)} %select_bitcast_fusion.2), channel_id=1, replica_groups=mesh['ray'=16,'tile'=8] {'tile'}, dimensions={1} | all-to-all | bytes 4194304 | tf_op jit(solution)/shard_map/all_to_all | solution.py:30
  758.8 6.1 fusion.39
  767.4 64.7 %psum.37 = f32[64]{0:T(128)S(1)} all-reduce(f32[64]{0:T(128)S(1)} %get-tuple-element.9), channel_id=1, replica_groups=mesh['ray'=16,'tile'=8] {'ray','tile'}, use_global_device_ids=true, to_apply=%region_6.0 | all-reduce | flops 64 | bytes 512 | tf_op jit(solution)/shard_map/psum | solution.py:62
  837.9 30.1 %all_to_all.31 = bf16[64,32,512]{2,0,1:T(8,128)(2,1)S(1)} all-to-all(bf16[64,32,512]{2,0,1:T(8,128)(2,1)S(1)} %convert_bitcast_fusion), channel_id=1, replica_groups=mesh['ray'=16,'tile'=8] {'tile'}, dimensions={1} | all-to-all | bytes 4194304 | tf_op jit(solution)/shard_map/all_to_all | solution.py:48
  872.4 6.2 all_gather_reshape.7
  878.6 535.9 %all-gather.5.cloned.1.call-done = f32[16,64,24576]{2,1,0:T(8,128)} async-done(((f32[1,64,24576]{2,1,0:T(8,128)}), f32[16,64,24576]{2,1,0:T(8,128)}) %all-gather.5.cloned.1.call-update) | async-done | bytes 100663312 | tf_op jit(solution)/shard_map/all_gather | solution.py:52
  1414.5 33.5 %reduce_sum.72 = f32[64,24576]{1,0:T(8,128)} reduce(f32[16,64,24576]{2,1,0:T(8,128)} %all-gather.5.cloned.1.call-done, f32[]{:T(128)} %constant.18.clone.1), dimensions={0}, to_apply=%region_7.10 | reduce | flops 23592960 | bytes 106954752 | tf_op jit(solution)/shard_map/reduce_sum | solution.py:53
  1448.0 5.8 multiply_reduce_fusion
  1453.8 12.4 psum.38
  1475.7 31.7 %all_to_all.32 = bf16[64,32,512]{2,0,1:T(8,128)(2,1)S(1)} all-to-all(bf16[64,32,512]{2,0,1:T(8,128)(2,1)S(1)} %select_bitcast_fusion.1), channel_id=1, replica_groups=mesh['ray'=16,'tile'=8] {'tile'}, dimensions={1} | all-to-all | bytes 4194304 | tf_op jit(solution)/shard_map/all_to_all | solution.py:30
  1507.4 6.1 fusion.40
  1516.0 64.7 %psum.39 = f32[64]{0:T(128)S(1)} all-reduce(f32[64]{0:T(128)S(1)} %multiply_reduce_fusion.2), channel_id=1, replica_groups=mesh['ray'=16,'tile'=8] {'ray','tile'}, use_global_device_ids=true, to_apply=%region_11.14 | all-reduce | flops 64 | bytes 512 | tf_op jit(solution)/shard_map/psum | solution.py:62
  1580.7 5.8 add_convert_fusion
  1596.1 7.3 multiply_add_fusion
  1603.4 19.0 %all-to-all-done.5 = bf16[64,32,512]{2,0,1:T(8,128)(2,1)S(1)} async-done(((bf16[64,32,512]{2,0,1:T(8,128)(2,1)}), bf16[64,32,512]{2,0,1:T(8,128)(2,1)S(1)}, u32[]{:S(2)}, u32[]{:S(2)}) %all-to-all-start.5) | async-done | bytes 2097184 | tf_op jit(solution)/shard_map/all_to_all | solution.py:30
  1622.4 6.0 fusion.41
  (61 shorter events, 63.3 us)
Async XLA Ops:
  8.5 83.9 %all-to-all-start = ((s32[1,8,4]{2,0,1:T(1,128)}), s32[1,8,4]{2,0,1:T(1,128)S(1)}, u32[]{:S(2)}, u32[]{:S(2)}) async-start(s32[1,8,4]{2,0,1:T(1,128)} %copy.21), calls=%async_computation | async-start | bytes 8192 | tf_op jit(solution)/shard_map/all_to_all | solution.py:17
  92.4 30.8 %all-to-all-start.1 = ((bf16[64,32,512]{2,0,1:T(8,128)(2,1)}), bf16[64,32,512]{2,0,1:T(8,128)(2,1)S(1)}, u32[]{:S(2)}, u32[]{:S(2)}) async-start(bf16[64,32,512]{2,0,1:T(8,128)(2,1)} %convert_bitcast_fusion.1), calls=%async_computation.1 | async-start | bytes 4194304 | tf_op jit(solution)/shard_map/all_to_all | solution.py:48
  96.8 573.3 %all-gather.3.cloned.1.call-start = ((), (), s32[]{:S(2)}) async-start(), calls=%async_computation.6 | async-start | bytes 106954752 | tf_op jit(solution)/shard_map/all_gather | solution.py:52
  133.8 1280.7 %all-gather.5.cloned.1.call-start = ((), (), s32[]{:S(2)}) async-start(), calls=%async_computation.7 | async-start | bytes 106954752 | tf_op jit(solution)/shard_map/all_gather | solution.py:52
  758.8 8.2 copy-start
  767.4 64.9 %copy-start.2 = (f32[64,2048]{1,0:T(8,128)}, f32[64,2048]{1,0:T(8,128)S(1)}, u32[]{:S(2)}) copy-start(f32[64,2048]{1,0:T(8,128)S(1)} %get-tuple-element.10) | copy-start | bytes 1572868
  1507.4 8.2 copy-start.3
  1591.7 30.7 %all-to-all-start.5 = ((bf16[64,32,512]{2,0,1:T(8,128)(2,1)}), bf16[64,32,512]{2,0,1:T(8,128)(2,1)S(1)}, u32[]{:S(2)}, u32[]{:S(2)}) async-start(bf16[64,32,512]{2,0,1:T(8,128)(2,1)} %select_bitcast_fusion), calls=%async_computation.5 | async-start | bytes 4194304 | tf_op jit(solution)/shard_map/all_to_all | solution.py:30
  1603.4 27.2 %copy-start.1 = (f32[64,2048]{1,0:T(8,128)S(1)}, f32[64,2048]{1,0:T(8,128)}, u32[]{:S(2)}) copy-start(f32[64,2048]{1,0:T(8,128)} %param.8) | copy-start | bytes 1572868
Sparse Core Ops, SparseCore 0:
  133.9 536.1 all-gather.2
  878.8 535.7 all-gather.4
